TPU v7x, 128 devices: a whole 4x4x4 slice. The times are simulated.
128 devices in a mesh: grp: 4 (over y), dev: 32 (over z, x, core).
Axes of the slice: x: 4, y: 4, z: 4, core: 2. Of those that a mesh axis runs over, the one named last changes fastest.
Arguments:
- points: float32 [3, 65536], P(None, 'dev'), may hold values from 0 to 1
- omega: bfloat16 [65536, 256], P('dev'), may hold values from -0.0234375 to 0.0234375
- pivots: int32 [32, 256], replicated, may hold values from 0 to 2047, as said below
- ranks: int32 [32], replicated, may hold values from 128 to 256, as said below
- owners: int32 [16], replicated, may hold values from 0 to 3, as said below
Outputs:
- interp: float32 [65536, 256], P(('grp', 'dev'))
- parent_samples: float32 [4, 8, 512, 256], P('grp', None, 'dev')
Inputs may be any that keep to these rules, and one draw needn't show every extreme that they name: The 256 pivots of a leaf are distinct. `ranks`: some leaf has exactly 256 skeleton rows in every draw. `owners`: no owner holds more than 8 parents, and some owner holds exactly 8.
All inputs are finite; a program needn't handle non-finite values.
Results may differ from a plain program's by a relative error of at most 0.0097.
Values may be sent and summed in bfloat16 or wider, within the bound.
A program may use at most 192 MiB of HBM per device.

v0:
```python
import math

import jax
import jax.numpy as jnp
from jax import lax
from jax.sharding import PartitionSpec as P

soften = 0.0001
highest = lax.Precision.HIGHEST


def copy_for_each(value, axis):
    copies = jnp.broadcast_to(value, (lax.axis_size(axis), *value.shape))
    return lax.all_to_all(copies, axis, split_axis=0, concat_axis=0, tiled=True)


def joined_along(parts, dim):
    parts = jnp.moveaxis(parts, 0, dim)
    lengths = parts.shape
    return parts.reshape(*lengths[:dim], lengths[dim] * lengths[dim + 1], *lengths[dim + 2 :])


def gathered_copies(value, axis, dim):
    parts = copy_for_each(value, axis)
    return joined_along(parts, dim)


def in_blocks(value, dim, peers):
    before, after = (value.shape[:dim], value.shape[dim + 1 :])
    return jnp.moveaxis(value.reshape(*before, peers, -1, *after), dim, 0)


def sum_at_owner(value, axis, dim):
    parts = in_blocks(value, dim, lax.axis_size(axis))
    arrived = lax.all_to_all(parts, axis, split_axis=0, concat_axis=0, tiled=True)
    return arrived.sum(axis=0)


def shifted(block, axis, distance):
    devices = range(lax.axis_size(axis))
    route = [(i - distance, i) for i in devices if i - distance in devices]
    return lax.ppermute(block, axis, route)


def kernel_block(row_pts, col_pts):
    dist_sq = (row_pts[0][:, None] - col_pts[0][None, :]) ** 2
    dist_sq = dist_sq + (row_pts[1][:, None] - col_pts[1][None, :]) ** 2
    dist_sq = dist_sq + (row_pts[2][:, None] - col_pts[2][None, :]) ** 2
    return 1.0 / jnp.sqrt(dist_sq + soften)


def body(points, omega, pivots, ranks, owners):
    groups = lax.axis_size("grp")
    devices = lax.axis_size("dev")
    group_id = lax.axis_index("grp")
    device_id = lax.axis_index("dev")
    leaf_size = omega.shape[0]
    samples_n = omega.shape[1]
    rank_max = pivots.shape[1]
    count_all = leaf_size * devices
    rows_group = count_all // groups
    slab_rows = leaf_size // groups
    leaves_group = devices // groups
    every_point = gathered_copies(points, "dev", 1)
    slab_start = group_id * rows_group + device_id * slab_rows
    my_leaf = slab_start // leaf_size
    slab_pts = lax.dynamic_slice_in_dim(every_point, slab_start, slab_rows, 1)
    start_sum = jnp.zeros((slab_rows, samples_n), jnp.float32)
    piece = lax.all_gather(omega, "dev", axis=0, tiled=True)
    piece_len = piece.shape[0]
    col_blk = math.gcd(piece_len, 2048)

    def one_block(number, running):
        first_col = number * col_blk
        col_pts = lax.dynamic_slice_in_dim(every_point, first_col, col_blk, 1)
        sketch = lax.dynamic_slice_in_dim(piece, number * col_blk, col_blk, 0)
        col_leaf = (first_col + jnp.arange(col_blk, dtype=jnp.int32)) // leaf_size
        kernel = kernel_block(slab_pts, col_pts)
        kernel = jnp.where(col_leaf[None, :] == my_leaf, 0.0, kernel).astype(jnp.bfloat16)
        return running + jnp.dot(kernel, sketch, preferred_element_type=jnp.float32)

    slab_samples = lax.fori_loop(0, piece_len // col_blk, one_block, start_sum)
    rank_ids = jnp.arange(rank_max, dtype=jnp.int32)
    local_leaf = device_id // groups
    within = slab_start - my_leaf * leaf_size
    my_pivots = pivots[my_leaf]
    my_live = rank_ids < ranks[my_leaf]
    slab_ids = jnp.arange(slab_rows, dtype=jnp.int32)
    picker = (my_pivots[:, None] - within == slab_ids[None, :]) & my_live[:, None]
    picked = jnp.dot(picker.astype(jnp.float32), slab_samples, precision=highest)
    sibling_leaf = jnp.bitwise_xor(device_id, 1)
    sib_pivots = pivots[sibling_leaf]
    sib_pts = every_point[:, sibling_leaf * leaf_size + sib_pivots]
    sib_kernel = kernel_block(sib_pts, points).astype(jnp.bfloat16)
    sib_live = (rank_ids < ranks[sibling_leaf]) & (device_id // leaves_group == group_id)
    correction = jnp.where(
        sib_live[:, None], jnp.dot(sib_kernel, omega, preferred_element_type=jnp.float32), 0.0
    )
    leaf_slots = jnp.arange(leaves_group, dtype=jnp.int32)
    skel_all = jnp.where((leaf_slots == local_leaf)[:, None, None], picked[None], 0.0)
    corr_all = jnp.where(
        (leaf_slots == sibling_leaf - group_id * leaves_group)[:, None, None], correction[None], 0.0
    )
    pairs_group = leaves_group // 2
    paired_part = (skel_all - corr_all).reshape(pairs_group, 2 * rank_max, samples_n)
    my_piece = sum_at_owner(paired_part, "dev", 1)
    position = device_id % groups
    skel_rows = picked
    for offset in range(1 - groups, groups):
        if offset != 0:
            arrived = shifted(picked, "dev", offset)
            source = position - offset
            skel_rows = skel_rows + jnp.where((source >= 0) & (source < groups), arrived, 0.0)
    gram_mat = jnp.dot(skel_rows, skel_rows.T, precision=highest)
    ridge_term = 0.1 * jnp.trace(gram_mat) / ranks[my_leaf].astype(jnp.float32) + 1e-06
    gram_mat = gram_mat + ridge_term * jnp.eye(rank_max, dtype=jnp.float32)
    factor = jnp.linalg.cholesky(gram_mat)
    right_side = jnp.dot(slab_samples, skel_rows.T, precision=highest)
    interp = jax.scipy.linalg.cho_solve((factor, True), right_side.T).T
    parent_count = owners.shape[0]
    slot_count = 2 * pairs_group
    parent_ids = jnp.arange(parent_count, dtype=jnp.int32)
    shared = owners[:, None] == owners[None, :]
    slot_of = jnp.sum(shared & (parent_ids[None, :] < parent_ids[:, None]), axis=1)
    slot_ids = jnp.arange(slot_count, dtype=jnp.int32)
    all_pieces = lax.all_gather(my_piece, "grp", axis=0, tiled=True)
    placing = (owners[None, :] == group_id) & (slot_ids[:, None] == slot_of[None, :])
    delivered = jnp.einsum(
        "sp,prk->srk", placing.astype(jnp.float32), all_pieces, precision=highest
    )
    return (interp, delivered[None])


def solution(mesh):
    placed = (P(None, "dev"), P("dev", None), P(), P(), P())
    return jax.shard_map(
        body,
        mesh=mesh,
        in_specs=placed,
        out_specs=(P(("grp", "dev"), None), P("grp", None, "dev", None)),
        check_vma=False,
    )
```

profile of v0, /device:TPU:2, one launch (start us, length us, event | category | flops | bytes accessed | tf_op | source)
XLA Modules:
  0.0 348.7 jit_solution(2332731837905459463)
XLA Ops:
  9.9 8.5 %all-to-all-start = ((f32[32,3,2048]{2,1,0:T(4,128)}), f32[32,3,2048]{2,1,0:T(4,128)S(1)}, u32[]{:S(2)}, u32[]{:S(2)}) async-start(f32[32,3,2048]{2,1,0:T(4,128)} %broadcast_in_dim.127), calls=%async_computation | async-start | bytes 2097152 | tf_op jit(solution)/shard_map/all_to_all | solution.py:14
  23.5 16.3 %all-to-all-done = f32[32,3,2048]{2,1,0:T(4,128)S(1)} async-done(((f32[32,3,2048]{2,1,0:T(4,128)}), f32[32,3,2048]{2,1,0:T(4,128)S(1)}, u32[]{:S(2)}, u32[]{:S(2)}) %all-to-all-start) | async-done | bytes 786464 | tf_op jit(solution)/shard_map/all_to_all | solution.py:14
  39.8 15.4 %copy.36 = f32[3,32,2048]{0,2,1:T(8,128)} copy(f32[3,32,2048]{2,0,1:T(4,128)S(1)} %bitcast.89) | data formatting | bytes 1572864 | tf_op jit(solution)/shard_map/transpose | solution.py:18
  55.2 19.8 %copy.38 = f32[3,65536]{1,0:T(4,128)S(1)} copy(f32[3,65536]{0,1:T(8,128)} %bitcast.84) | data formatting | bytes 1572864
  75.0 12.6 %gather_fusion = f32[256,3]{1,0:T(8,128)S(1)} fusion(f32[3,65536]{0,1:T(8,128)} %bitcast.85, s32[1024]{0:T(1024)S(1)} %pad_clamp_fusion), kind=kCustom, calls=%fused_computation | custom fusion | bytes 7168 | tf_op jit(solution)/shard_map/gather | solution.py:93
  89.0 43.1 %all-gather.2.cloned.1.call-done = bf16[65536,256]{1,0:T(8,128)(2,1)} async-done(((bf16[2048,256]{1,0:T(8,128)(2,1)}), bf16[65536,256]{1,0:T(8,128)(2,1)}) %all-gather.2.cloned.1.call-update) | async-done | bytes 33554448 | tf_op jit(solution)/shard_map/all_gather | solution.py:69
  132.1 98.0 %while.18 = (s32[]{:T(128)}, f32[512,256]{1,0:T(8,128)S(1)}, s32[]{:T(128)}, f32[3,512]{1,0:T(4,128)S(1)}, f32[3,65536]{1,0:T(4,128)S(1)}, /*index=5*/bf16[65536...) while((s32[]{:T(128)}, f32[512,256]{1,0:T(8,128)S(1)}, ...), condition=%wide.region_1.2_spmd.clone, body=%wide.region_0.1_spmd.clone.sunk | while | flops 548702208 | bytes 2193629 | solution.py:82
  132.3 3.0 fusion.72
  135.4 2.9 fusion.72
  138.5 2.9 fusion.72
  141.5 2.9 fusion.72
  147.6 2.9 fusion.72
  150.7 2.9 fusion.72
  159.9 2.9 fusion.72
  172.1 2.9 fusion.72
  178.2 2.9 fusion.72
  181.3 2.9 fusion.72
  193.5 2.9 fusion.72
  199.7 2.9 fusion.72
  202.7 2.9 fusion.72
  211.9 2.9 fusion.72
  215.0 2.9 fusion.72
  221.1 2.9 fusion.72
  239.9 3.6 %collective-permute-start.4 = (f32[256,256]{1,0:T(8,128)S(1)}, f32[256,256]{1,0:T(8,128)}, u32[]{:S(2)}, u32[]{:S(2)}) collective-permute-start(f32[256,256]{1,0:T(8,128)S(1)} %fusion.19), channel_id=1, source_target_pairs={{0,2},{1,3},{2,4},{3,5},{4,6},{5,7},{6,8},{7,9},{8,10},{9,11},{10,... | collective-permute-start | bytes 786440 | tf_op jit(solution)/shard_map/ppermute | solution.py:42
  243.5 7.7 %collective-permute-start.5 = (f32[256,256]{1,0:T(8,128)S(1)}, f32[256,256]{1,0:T(8,128)}, u32[]{:S(2)}, u32[]{:S(2)}) collective-permute-start(f32[256,256]{1,0:T(8,128)S(1)} %fusion.19), channel_id=1, source_target_pairs={{0,3},{1,4},{2,5},{3,6},{4,7},{5,8},{6,9},{7,10},{8,11},{9,12},{10... | collective-permute-start | bytes 786440 | tf_op jit(solution)/shard_map/ppermute | solution.py:42
  253.6 4.3 %all-to-all-start.1 = ((f32[32,4,16,256]{3,2,1,0:T(8,128)}), f32[32,4,16,256]{3,2,1,0:T(8,128)S(1)}, u32[]{:S(2)}, u32[]{:S(2)}) async-start(f32[32,4,16,256]{3,2,1,0:T(8,128)} %copy.40), calls=%async_computation.1 | async-start | bytes 4194304 | tf_op jit(solution)/shard_map/all_to_all | solution.py:35
  262.5 11.7 %cholesky.49 = f32[128,128]{1,0:T(8,128)S(1)} custom-call(f32[128,128]{1,0:T(8,128)S(1)} %cholesky.115), custom_call_target="Cholesky" | custom-call | tf_op jit(solution)/shard_map/jit(cholesky)/cholesky | solution.py:117
  274.3 9.8 %custom-call.18 = f32[1,128,128]{1,2,0:T(8,128)S(1)} custom-call(f32[1,128,128]{2,1,0:T(8,128)S(1)} %get-tuple-element.261), custom_call_target="InvertDiagBlocksLowerTriangular" | custom-call | tf_op jit(solution)/shard_map/jit(cholesky)/cholesky | solution.py:117
  286.3 11.7 %cholesky.103 = f32[128,128]{1,0:T(8,128)S(1)} custom-call(f32[128,128]{1,0:T(8,128)S(1)} %convolution_subtract_fusion.1), custom_call_target="Cholesky" | custom-call | tf_op jit(solution)/shard_map/jit(cholesky)/cholesky | solution.py:117
  300.1 3.9 %while.17 = (s32[]{:T(128)}, f32[256,256]{1,0:T(8,128)S(1)}, s32[2,2]{1,0:T(2,128)S(1)}, f32[2,128,128]{2,1,0:T(8,128)S(1)}, s32[]{:T(128)}) while((s32[]{:T(128)}, f32[256,256]{1,0:T(8,128)S(1)}, s32[2,2]{1,0:T(2,128)S(1)}, f32[2,128,128]{2,1,0:T(8,128)S(1)}, s32[]{:T(128)}) %tuple.89), condition=%wide.while_cond, body=%wide.while_body.sunk | while | flops 2 | bytes 131181 | solution.py:119
  304.1 19.9 %custom-call.19 = f32[2,128,128]{1,2,0:T(8,128)S(1)} custom-call(f32[2,128,128]{2,1,0:T(8,128)S(1)} %get-tuple-element.165), custom_call_target="InvertDiagBlocksLowerTriangular" | custom-call | tf_op jit(solution)/shard_map/jit(_cho_solve)/triangular_solve | solution.py:119
  328.2 12.6 %all_gather.7 = f32[16,16,256]{2,1,0:T(8,128)S(1)} all-gather(f32[4,16,256]{2,1,0:T(8,128)S(1)} %reduce_sum.30), channel_id=1, replica_groups=mesh['grp'=4,'dev'=32] {'grp'}, dimensions={0}, use_global_device_ids=true | all-gather | bytes 327680 | tf_op jit(solution)/shard_map/all_gather | solution.py:126
  (198 shorter events, 86.4 us)
Async XLA Ops:
  7.2 16.3 %copy-start.3 = (f32[3,2048]{1,0:T(4,128)S(1)}, f32[3,2048]{1,0:T(4,128)}, u32[]{:S(2)}) copy-start(f32[3,2048]{1,0:T(4,128)} %param.7) | copy-start | bytes 73732
  7.2 11.7 %copy-start.4 = (s32[32]{0:T(128)S(1)}, s32[32]{0:T(128)}, u32[]{:S(2)}) copy-start(s32[32]{0:T(128)} %param.10) | copy-start | bytes 388
  7.2 15.5 %copy-start.5 = (s32[16]{0:T(128)S(1)}, s32[16]{0:T(128)}, u32[]{:S(2)}) copy-start(s32[16]{0:T(128)} %param.11) | copy-start | bytes 196
  7.2 124.9 %all-gather.2.cloned.1.call-start = ((), (), s32[]{:S(2)}) async-start(), calls=%async_computation.2 | async-start | bytes 34603008 | tf_op jit(solution)/shard_map/all_gather | solution.py:69
  9.9 29.9 %all-to-all-start = ((f32[32,3,2048]{2,1,0:T(4,128)}), f32[32,3,2048]{2,1,0:T(4,128)S(1)}, u32[]{:S(2)}, u32[]{:S(2)}) async-start(f32[32,3,2048]{2,1,0:T(4,128)} %broadcast_in_dim.127), calls=%async_computation | async-start | bytes 2097152 | tf_op jit(solution)/shard_map/all_to_all | solution.py:14
  132.1 99.8 %copy-start = (bf16[2048,256]{1,0:T(8,128)(2,1)S(1)}, bf16[2048,256]{1,0:T(8,128)(2,1)}, u32[]{:S(2)}) copy-start(bf16[2048,256]{1,0:T(8,128)(2,1)} %param.8) | copy-start | bytes 3145732
  230.6 12.9 %collective-permute-start = (f32[256,256]{1,0:T(8,128)S(1)}, f32[256,256]{1,0:T(8,128)S(1)}, u32[]{:S(2)}, u32[]{:S(2)}) collective-permute-start(f32[256,256]{1,0:T(8,128)S(1)} %fusion.19), channel_id=1, source_target_pairs={{3,0},{4,1},{5,2},{6,3},{7,4},{8,5},{9,6},{10,7},{11,8},{12,9},{13... | collective-permute-start | bytes 786440 | tf_op jit(solution)/shard_map/ppermute | solution.py:42
  232.8 25.2 %collective-permute-start.1 = (f32[256,256]{1,0:T(8,128)S(1)}, f32[256,256]{1,0:T(8,128)S(1)}, u32[]{:S(2)}, u32[]{:S(2)}) collective-permute-start(f32[256,256]{1,0:T(8,128)S(1)} %fusion.19), channel_id=1, source_target_pairs={{2,0},{3,1},{4,2},{5,3},{6,4},{7,5},{8,6},{9,7},{10,8},{11,9},{12,... | collective-permute-start | bytes 786440 | tf_op jit(solution)/shard_map/ppermute | solution.py:42
  235.3 22.7 %collective-permute-start.2 = (f32[256,256]{1,0:T(8,128)S(1)}, f32[256,256]{1,0:T(8,128)}, u32[]{:S(2)}, u32[]{:S(2)}) collective-permute-start(f32[256,256]{1,0:T(8,128)S(1)} %fusion.19), channel_id=1, source_target_pairs={{1,0},{2,1},{3,2},{4,3},{5,4},{6,5},{7,6},{8,7},{9,8},{10,9},{11,1... | collective-permute-start | bytes 786440 | tf_op jit(solution)/shard_map/ppermute | solution.py:42
  237.2 20.8 %collective-permute-start.3 = (f32[256,256]{1,0:T(8,128)S(1)}, f32[256,256]{1,0:T(8,128)}, u32[]{:S(2)}, u32[]{:S(2)}) collective-permute-start(f32[256,256]{1,0:T(8,128)S(1)} %fusion.19), channel_id=1, source_target_pairs={{0,1},{1,2},{2,3},{3,4},{4,5},{5,6},{6,7},{7,8},{8,9},{9,10},{10,1... | collective-permute-start | bytes 786440 | tf_op jit(solution)/shard_map/ppermute | solution.py:42
  239.9 18.1 %collective-permute-start.4 = (f32[256,256]{1,0:T(8,128)S(1)}, f32[256,256]{1,0:T(8,128)}, u32[]{:S(2)}, u32[]{:S(2)}) collective-permute-start(f32[256,256]{1,0:T(8,128)S(1)} %fusion.19), channel_id=1, source_target_pairs={{0,2},{1,3},{2,4},{3,5},{4,6},{5,7},{6,8},{7,9},{8,10},{9,11},{10,... | collective-permute-start | bytes 786440 | tf_op jit(solution)/shard_map/ppermute | solution.py:42
  243.5 15.2 %collective-permute-start.5 = (f32[256,256]{1,0:T(8,128)S(1)}, f32[256,256]{1,0:T(8,128)}, u32[]{:S(2)}, u32[]{:S(2)}) collective-permute-start(f32[256,256]{1,0:T(8,128)S(1)} %fusion.19), channel_id=1, source_target_pairs={{0,3},{1,4},{2,5},{3,6},{4,7},{5,8},{6,9},{7,10},{8,11},{9,12},{10... | collective-permute-start | bytes 786440 | tf_op jit(solution)/shard_map/ppermute | solution.py:42
  253.6 74.4 %all-to-all-start.1 = ((f32[32,4,16,256]{3,2,1,0:T(8,128)}), f32[32,4,16,256]{3,2,1,0:T(8,128)S(1)}, u32[]{:S(2)}, u32[]{:S(2)}) async-start(f32[32,4,16,256]{3,2,1,0:T(8,128)} %copy.40), calls=%async_computation.1 | async-start | bytes 4194304 | tf_op jit(solution)/shard_map/all_to_all | solution.py:35
  258.0 0.7 copy-start.2
  259.9 40.1 %copy-start.6 = (s32[2]{0:T(128)S(1)}, s32[2]{0:T(128)}, u32[]{:S(2)}) copy-start(s32[2]{0:T(128)} %iota_multiply_fusion) | copy-start | bytes 28
  261.8 0.7 copy-start.1
Sparse Core Ops, SparseCore 0:
  10.3 121.8 all-gather.1
where the time goes:
time: 355 us; the launch traced here: 349 us
  matrix products  100 us (28%)
  local copies, waits for them, and re-layouts  64.6 us (18%)
  waiting for transfers between devices  60.1 us (17%)
  other arithmetic  59.7 us (17%)
  starting transfers between devices  32.5 us (9%)
  between operations  17.2 us (5%)
  blocking collectives  12.6 us (4%)
    dot_general x32, matrix products, one_block(): return running + jnp.dot(kernel, sketch, preferred_element_type=jnp.float32)  92.2 us
    all_gather x1, waiting for transfers between devices, body(): piece = lax.all_gather(omega, 'dev', axis=0, tiled=True)  43.1 us
    another operation x6, other arithmetic, body(): factor = jnp.linalg.cholesky(gram_mat)  34 us
    unnamed x18, local copies, waits for them, and re-layouts  23 us
    another operation x3, other arithmetic, body(): interp = jax.scipy.linalg.cho_solve((factor, True), right_side.T).T  20.5 us
    ppermute x6, starting transfers between devices, shifted(): return lax.ppermute(block, axis, route)  19.7 us
    all_to_all x1, waiting for transfers between devices, copy_for_each(): return lax.all_to_all(copies, axis, split_axis=0, concat_axis=0, tiled=True)  16.3 us
    transpose x1, local copies, waits for them, and re-layouts, joined_along(): parts = jnp.moveaxis(parts, 0, dim)  15.4 us
  transfers between devices with their start and end apart: 9, of which 2 were waited for; matrix products, arithmetic and copies ran while one was open for 36% of the time, Pallas kernels for 0%

commit v1 on v0

v1 whole, which is shorter than its diff:
```python
import functools

import jax
import jax.numpy as jnp
from jax import lax
from jax.experimental import pallas as pl
from jax.experimental.pallas import tpu as pltpu
from jax.sharding import PartitionSpec as P

BF = jnp.bfloat16
F32 = jnp.float32
MESH = pl.DeviceIdType.MESH
HIGHEST = lax.Precision.HIGHEST
SOFTEN = 0.0001
DEPTH = 32
WAYS = 4
LEAF = 2048
SLAB = 512
S = 256
RMAX = 256
PIECE = 64
HALF = 1024


def place():
    y = lax.axis_index("grp")
    d = lax.axis_index("dev")
    return y, d // 8, (d // 2) % 4, d % 2


def dev_of(z, x, c):
    return ((z % 4) * 4 + (x % 4)) * 2 + c


SPLIT_PAIRS = [(0, 0), (0, 1), (1, 0), (1, 1), (0, 2), (2, 0), (1, 2), (2, 1)]


def splits(value):
    high = value.astype(BF).astype(F32)
    rest = value - high
    mid = rest.astype(BF).astype(F32)
    return [high, mid, rest - mid]


def distance_rows(coords, col_side):
    n = coords.shape[1]
    row = lax.broadcasted_iota(jnp.int32, (8, n), 0)
    norm = jnp.sum(coords * coords, axis=0, keepdims=True)
    twice = coords + pltpu.roll(coords, 3, 0)
    if col_side:
        value = jnp.where(row < 6, -2.0 * twice, jnp.where(row == 6, 1.0, norm + SOFTEN))
    else:
        value = jnp.where(row < 6, twice, jnp.where(row == 6, norm, 1.0))
    parts = splits(value)
    side, varying = (1, 7) if col_side else (0, 6)
    blocks = []
    for g in range(4):
        first, second = SPLIT_PAIRS[2 * g][side], SPLIT_PAIRS[2 * g + 1][side]
        block = jnp.where(row < 3, parts[first], parts[second])
        if g < 3:
            block = jnp.where(row >= 6, jnp.where(row == varying, parts[g], 1.0), block)
        else:
            block = jnp.where(row >= 6, 0.0, block)
        blocks.append(block)
    return jnp.concatenate(blocks, axis=0)


def centred(block):
    n = block.shape[1]
    return jnp.concatenate([block - 0.5, jnp.zeros((5, n), F32)], axis=0)


def sweep_kernel(
    pts, om_in, pivots, ranks,
    s_out, skel_out, par_out,
    cp, rp, om, arow, apiv, bcol, acc, accp, kb0, kb1, sbuf, rbuf, prbuf, skel, red, par,
    own_sem, cps, cpr, rps, rpr, oms, omr, fws, rds, rdr, pvs, pvr, sks, skr, pas, par_sem,
):
    y, z, x, c = place()
    dirs = [(1, 0), (0, 1), (0, 3)]

    def block_chip(j):
        return (x + j) % 4, (z + 2 * (j % 2)) % 4

    def block_leaf(j):
        xr, zr = block_chip(j)
        return y * 8 + 2 * zr + xr // 2

    def to(dev, grp=None):
        return (y if grp is None else grp, dev)

    me = dev_of(z, x, c)
    own_copy = pltpu.make_async_copy(om_in, om.at[0], own_sem)
    own_copy.start()
    barrier = pltpu.get_barrier_semaphore()
    for k in range(1, 32):
        pl.semaphore_signal(barrier, inc=1, device_id=to((me + k) % 32), device_id_type=MESH)
    for gy in range(1, 4):
        for zs in range(4):
            pl.semaphore_signal(
                barrier, inc=1, device_id=to(dev_of(zs, z, x // 2), (y + gy) % 4), device_id_type=MESH
            )
    cp[0] = pts[...]
    pl.semaphore_wait(barrier, 43)

    def row_copy(i, j, core):
        xr, zr = 2 * c + i, x
        return pltpu.make_async_remote_copy(
            src_ref=pts, dst_ref=rp.at[j], send_sem=rps.at[i * 8 + j * 2 + core], recv_sem=rpr.at[j],
            device_id=to(dev_of(zr - 2 * (j % 2) + 4, xr - j + 4, core)), device_id_type=MESH,
        )

    def row_target(i, j, core):
        return dev_of(x - 2 * (j % 2) + 4, 2 * c + i - j + 4, core)

    @pl.when(z == y)
    def _():
        for i in range(2):
            for j in range(WAYS):
                for core in range(2):
                    self_target = row_target(i, j, core) == me

                    @pl.when(self_target)
                    def _():
                        pltpu.make_async_copy(pts, rp.at[j], rpr.at[j]).start()

                    @pl.when(jnp.logical_not(self_target))
                    def _():
                        row_copy(i, j, core).start()

    def col_copies():
        copies = [
            pltpu.make_async_remote_copy(
                src_ref=pts, dst_ref=cp.at[1], send_sem=cps.at[0], recv_sem=cpr.at[1],
                device_id=to(dev_of(z, x, 1 - c)), device_id_type=MESH,
            )
        ]
        for i, (dx, dz) in enumerate(dirs):
            for other in range(2):
                core = c if other == 0 else 1 - c
                copies.append(
                    pltpu.make_async_remote_copy(
                        src_ref=pts, dst_ref=cp.at[2 + 2 * i + other],
                        send_sem=cps.at[1 + 2 * i + other], recv_sem=cpr.at[2 + 2 * i + other],
                        device_id=to(dev_of(z - dz + 4, x - dx + 4, core)), device_id_type=MESH,
                    )
                )
        return copies

    col_sends = col_copies()
    for copy in col_sends:
        copy.start()

    def om_send(i, half):
        rows = pl.ds(half * HALF, HALF)
        if i == 0:
            slot, dev = 1, dev_of(z, x, 1 - c)
        else:
            dx, dz = dirs[i - 1]
            slot, dev = 2 * i, dev_of(z - dz + 4, x - dx + 4, c)
        return pltpu.make_async_remote_copy(
            src_ref=om_in.at[rows], dst_ref=om.at[slot, rows], send_sem=oms.at[i, half],
            recv_sem=omr.at[slot, half], device_id=to(dev), device_id_type=MESH,
        )

    for half in range(2):
        for i in range(4):
            om_send(i, half).start()

    def forward(slot, half):
        rows = pl.ds(half * HALF, HALF)
        return pltpu.make_async_remote_copy(
            src_ref=om.at[slot, rows], dst_ref=om.at[slot + 1, rows], send_sem=fws.at[slot // 2 - 1, half],
            recv_sem=omr.at[slot + 1, half], device_id=to(dev_of(z, x, 1 - c)), device_id_type=MESH,
        )

    def om_arrived(slot, half):
        rows = pl.ds(half * HALF, HALF)
        pltpu.make_async_copy(om.at[slot, rows], om.at[slot, rows], omr.at[slot, half]).wait()

    def build_col(slot):
        bcol[slot] = distance_rows(centred(cp[slot]), True).astype(BF)

    build_col(0)

    pick_acc = [jnp.zeros((8, 128), F32), jnp.zeros((8, 128), F32)]
    for j in range(WAYS):
        pltpu.make_async_copy(rp.at[j], rp.at[j], rpr.at[j]).wait()
        xr, zr = block_chip(j)
        start = pl.multiple_of(((xr % 2) * 2 + c) * SLAB, SLAB)
        arow[j] = distance_rows(centred(rp[j, :, pl.ds(start, SLAB)]), False).T.astype(BF)
        whole = centred(rp[j])
        split = jnp.concatenate([*splits(whole), jnp.zeros((8, LEAF), F32)], axis=0).astype(BF)
        piv = jnp.broadcast_to(pivots[pl.ds(block_leaf(j), 1), :], (8, RMAX))
        piv = jnp.where(xr % 2 == 0, piv[:, :128], piv[:, 128:])
        piv = jnp.where(c == j % 2, piv, pltpu.roll(piv, 64, 1))
        lane = lax.broadcasted_iota(jnp.int32, (8, 128), 1)
        piv = jnp.where(lane // 64 == j % 2, piv, -1)
        here = lax.broadcasted_iota(jnp.int32, (LEAF, 128), 0) == piv[:1]
        hit = jnp.dot(split, here.astype(BF), preferred_element_type=F32)
        pick_acc[j // 2] = pick_acc[j // 2] + (hit[0:8] + hit[8:16] + hit[16:24])
    for t in range(2):
        apiv[t * 128 : (t + 1) * 128] = distance_rows(pick_acc[t], False).T.astype(BF)
    for slot in range(1, 8):
        pltpu.make_async_copy(cp.at[slot], cp.at[slot], cpr.at[slot]).wait()
        build_col(slot)
    own_copy.wait()

    acc[...] = jnp.zeros_like(acc)
    accp[...] = jnp.zeros_like(accp)

    def nth(i):
        k = (i - 4) % 6
        late = i >= 4
        slot = jnp.where(late, jnp.where(k < 3, 2 + 2 * k, 3 + 2 * (k - 3)), i // 2)
        half = jnp.where(late, (i - 4) // 6, i % 2)
        return slot, half

    def slot_leaf(slot):
        pair = slot // 2
        xq = jnp.where(pair == 1, x + 1, x) % 4
        zq = (z + jnp.where(pair == 2, 1, jnp.where(pair == 3, 3, 0))) % 4
        cq = jnp.where(slot % 2 == 0, c, 1 - c)
        return dev_of(zq, xq, cq)

    def gen(rows, slot, half, kb):
        cols = pl.ds(pl.multiple_of(half * HALF, HALF), HALF)
        dist = jnp.dot(rows, bcol[slot, :, cols], preferred_element_type=F32)
        kb[...] = lax.rsqrt(dist).astype(BF)

    def product(slot, half, kb):
        rows = pl.ds(pl.multiple_of(half * HALF, HALF), HALF)
        return jnp.dot(kb[...], om[slot, rows, :], preferred_element_type=F32)

    def use_main(slot, half, j, kb):
        keep = jnp.where(slot_leaf(slot) == block_leaf(j), 0.0, 1.0).astype(F32)
        acc[j] += keep * product(slot, half, kb)

    def ready(i):
        slot, half = nth(i)

        @pl.when(i >= 2)
        def _():
            om_arrived(slot, half)

        @pl.when(jnp.logical_and(slot >= 2, slot % 2 == 0))
        def _():
            forward(slot, half).start()

    gen(arow[0], 0, 0, kb0)

    @pl.loop(0, 20)
    def _(t):
        i = t // 2
        j = (t % 2) * 2
        slot, half = nth(i)

        @pl.when(t % 2 == 0)
        def _():
            ready(i)

        gen(arow[j + 1], slot, half, kb1)
        use_main(slot, half, j, kb0)
        nxt = jnp.minimum(t + 1, 19)
        nslot, nhalf = nth(nxt // 2)
        gen(arow[(nxt % 2) * 2], nslot, nhalf, kb0)
        use_main(slot, half, j + 1, kb1)

    for i in range(10, 13):
        ready(jnp.int32(i))
    kp0, kp1 = kb0.at[pl.ds(0, RMAX)], kb1.at[pl.ds(0, RMAX)]

    def use_piv(slot, half, kb):
        got = product(slot, half, kb)
        for j in range(WAYS):
            own = slot_leaf(slot) == block_leaf(j)
            sib = dev_of(slot_leaf(slot) // 8, (slot_leaf(slot) // 2) % 4, 1 - slot_leaf(slot) % 2) == block_leaf(j)
            part = got[j * PIECE : (j + 1) * PIECE]
            accp[j, 0] += jnp.where(jnp.logical_or(own, sib), 0.0, 1.0).astype(F32) * part
            accp[j, 1] += jnp.where(sib, 1.0, 0.0).astype(F32) * part

    gen(apiv[...], 0, 0, kp0)

    @pl.loop(0, 8)
    def _(t):
        @pl.when(t >= 6)
        def _():
            for e in range(2):
                @pl.when(2 * t + e >= 13)
                def _():
                    slot, half = nth(2 * t + e)
                    om_arrived(slot, half)

        slot, half = nth(2 * t)
        slot1, half1 = nth(2 * t + 1)
        gen(apiv[...], slot1, half1, kp1)
        use_piv(slot, half, kp0)
        slot2, half2 = nth(jnp.minimum(2 * t + 2, 15))
        gen(apiv[...], slot2, half2, kp0)
        use_piv(slot1, half1, kp1)

    def piv_send(j):
        xr, zr = block_chip(j)
        return pltpu.make_async_remote_copy(
            src_ref=accp.at[j], dst_ref=prbuf.at[j - 1], send_sem=pvs.at[j - 1], recv_sem=pvr.at[j - 1],
            device_id=to(dev_of(zr, xr, c)), device_id_type=MESH,
        )

    for j in range(1, WAYS):
        piv_send(j).start()

    def main_send(j):
        xr, zr = block_chip(j)
        return pltpu.make_async_remote_copy(
            src_ref=sbuf.at[j - 1], dst_ref=rbuf.at[j - 1], send_sem=rds.at[j - 1], recv_sem=rdr.at[j - 1],
            device_id=to(dev_of(zr, xr, c)), device_id_type=MESH,
        )

    piece = 2 * (x % 2) + c
    piece_rows = pl.ds(pl.multiple_of(piece * PIECE, PIECE), PIECE)

    def skel_send(k):
        xs = x if k == 0 else x + 1 - 2 * (x % 2)
        core = 1 - c if k != 1 else c
        return pltpu.make_async_remote_copy(
            src_ref=skel.at[piece_rows], dst_ref=skel.at[piece_rows], send_sem=sks.at[k], recv_sem=skr.at[k],
            device_id=to(dev_of(z, xs, core)), device_id_type=MESH,
        )

    def par_dev(k):
        return dev_of(x, 2 * c + k // 2, k % 2)

    def par_send(k, g):
        return pltpu.make_async_remote_copy(
            src_ref=red.at[pl.ds(k * 16, 16)], dst_ref=par.at[4 * y + z], send_sem=pas.at[4 * g + k],
            recv_sem=par_sem.at[4 * y + z], device_id=to(par_dev(k), (y + g) % 4), device_id_type=MESH,
        )

    def finish_pivots():
        for j in range(3):
            pltpu.make_async_copy(prbuf.at[j], prbuf.at[j], pvr.at[j]).wait()
        total = accp[0] + prbuf[0] + prbuf[1] + prbuf[2]
        ids = lax.broadcasted_iota(jnp.int32, (PIECE, S), 0) + piece * PIECE
        live = ids < ranks[block_leaf(0)]
        skel[piece_rows, :] = jnp.where(live, total[0] + total[1], 0.0)
        red[...] = jnp.where(live, total[0], 0.0)
        for k in range(3):
            skel_send(k).start()
        for k in range(4):
            for g in range(4):
                if g:
                    par_send(k, g).start()
                else:
                    self_target = par_dev(k) == me

                    @pl.when(self_target)
                    def _():
                        pltpu.make_async_copy(
                            red.at[pl.ds(k * 16, 16)], par.at[4 * y + z], par_sem.at[4 * y + z]
                        ).start()

                    @pl.when(jnp.logical_not(self_target))
                    def _():
                        par_send(k, g).start()

    gen(arow[1], 2, 1, kb0)

    @pl.loop(0, 12)
    def _(t):
        j = (t // 3 + 1) % 4
        i = 10 + 2 * (t % 3)

        @pl.when(t == 4)
        def _():
            finish_pivots()

        slot, half = nth(i)
        slot1, half1 = nth(i + 1)
        gen(arow[j], slot1, half1, kb1)
        use_main(slot, half, j, kb0)
        nxt = jnp.minimum(t + 1, 11)
        slot2, half2 = nth(10 + 2 * (nxt % 3))
        gen(arow[(nxt // 3 + 1) % 4], slot2, half2, kb0)
        use_main(slot1, half1, j, kb1)
        for jj in range(1, WAYS):
            @pl.when(t == 3 * jj - 1)
            def _():
                sbuf[jj - 1] = acc[jj].astype(BF)
                main_send(jj).start()

    for j in range(3):
        pltpu.make_async_copy(rbuf.at[j], rbuf.at[j], rdr.at[j]).wait()
    s_out[...] = acc[0] + (rbuf[0].astype(F32) + rbuf[1].astype(F32)) + rbuf[2].astype(F32)
    for k in range(3):
        pltpu.make_async_copy(skel.at[pl.ds(0, PIECE)], skel.at[pl.ds(0, PIECE)], skr.at[k]).wait()
    skel_out[...] = skel[...]
    for q in range(16):
        pltpu.make_async_copy(par.at[q], par.at[q], par_sem.at[q]).wait()
    par_out[...] = par[...]

    @pl.when(z == y)
    def _():
        for i in range(2):
            for j in range(WAYS):
                for core in range(2):
                    @pl.when(row_target(i, j, core) != me)
                    def _():
                        row_copy(i, j, core).wait_send()

    for copy in col_sends:
        copy.wait_send()
    for half in range(2):
        for i in range(4):
            om_send(i, half).wait_send()
        for i in range(3):
            forward(2 + 2 * i, half).wait_send()
    for j in range(1, WAYS):
        piv_send(j).wait_send()
        main_send(j).wait_send()
    for k in range(3):
        skel_send(k).wait_send()
    for k in range(4):
        for g in range(4):
            if g:
                par_send(k, g).wait_send()
            else:
                @pl.when(par_dev(k) != me)
                def _():
                    par_send(k, g).wait_send()


def hdot(a, b, dims):
    return lax.dot_general(a, b, (dims, ((), ())), precision=HIGHEST, preferred_element_type=F32)


def solve_kernel(samples, skel, par, ranks, owners, interp, placed):
    y, z, x, c = place()
    rows = skel[...]
    gram = hdot(rows, rows, ((1,), (1,)))
    squares = jnp.sum(rows * rows, axis=1, keepdims=True)
    trace = jnp.sum(squares, axis=0, keepdims=True)
    rank = ranks[y * 8 + 2 * z + x // 2].astype(F32)
    low = 0.1 * trace / rank + 1e-06
    eye = lax.broadcasted_iota(jnp.int32, (RMAX, RMAX), 0) == lax.broadcasted_iota(jnp.int32, (RMAX, RMAX), 1)
    gram = gram + jnp.where(eye, low, 0.0)
    high = low + trace
    a = 2.0 / (low + high)
    ratio = low / high
    inv = None
    for step in range(9):
        gap = (1.0 - ratio) / (1.0 + ratio)
        grow = 2.0 / (2.0 - gap * gap)
        if inv is None:
            inv = grow * (jnp.where(eye, 2.0 * a, 0.0) - a * a * gram)
        else:
            prod = hdot(gram, inv, ((1,), (0,)))
            inv = grow * hdot(inv, jnp.where(eye, 2.0, 0.0) - prod, ((1,), (0,)))
        ratio = 1.0 - gap * gap
    basis = hdot(inv, rows, ((1,), (0,)))
    interp[...] = hdot(samples[...], basis, ((1,), (1,)))
    placed[...] = jnp.zeros_like(placed)
    count = jnp.int32(0)
    for q in range(16):
        mine = owners[q] == y

        @pl.when(mine)
        def _():
            placed[0, count] = par[q]

        count = count + jnp.where(mine, 1, 0)


def body(points, omega, pivots, ranks, owners):
    vmem = pl.BlockSpec(memory_space=pltpu.VMEM)
    smem = pl.BlockSpec(memory_space=pltpu.SMEM)
    dma = pltpu.SemaphoreType.DMA
    samples, skel, par = pl.pallas_call(
        sweep_kernel,
        name="sweep",
        out_shape=[
            jax.ShapeDtypeStruct((SLAB, S), F32),
            jax.ShapeDtypeStruct((RMAX, S), F32),
            jax.ShapeDtypeStruct((16, 16, S), F32),
        ],
        in_specs=[vmem, pl.BlockSpec(memory_space=pl.ANY), vmem, smem],
        out_specs=[vmem, vmem, vmem],
        scratch_shapes=[
            pltpu.VMEM((8, 3, LEAF), F32),
            pltpu.VMEM((4, 3, LEAF), F32),
            pltpu.VMEM((8, LEAF, S), BF),
            pltpu.VMEM((4, SLAB, DEPTH), BF),
            pltpu.VMEM((RMAX, DEPTH), BF),
            pltpu.VMEM((8, DEPTH, LEAF), BF),
            pltpu.VMEM((4, SLAB, S), F32),
            pltpu.VMEM((4, 2, PIECE, S), F32),
            pltpu.VMEM((SLAB, HALF), BF),
            pltpu.VMEM((SLAB, HALF), BF),
            pltpu.VMEM((3, SLAB, S), BF),
            pltpu.VMEM((3, SLAB, S), BF),
            pltpu.VMEM((3, 2, PIECE, S), F32),
            pltpu.VMEM((RMAX, S), F32),
            pltpu.VMEM((PIECE, S), F32),
            pltpu.VMEM((16, 16, S), F32),
            dma, dma((7,)), dma((8,)), dma((16,)), dma((4,)), dma((4, 2)), dma((8, 2)), dma((3, 2)),
            dma((3,)), dma((3,)), dma((3,)), dma((3,)), dma((3,)), dma((3,)), dma((16,)), dma((16,)),
        ],
        compiler_params=pltpu.CompilerParams(
            collective_id=0, has_side_effects=True, vmem_limit_bytes=56 * 2**20
        ),
    )(points, omega, pivots, ranks)
    interp, placed = pl.pallas_call(
        solve_kernel,
        name="solve",
        out_shape=[
            jax.ShapeDtypeStruct((SLAB, RMAX), F32),
            jax.ShapeDtypeStruct((1, 8, 16, S), F32),
        ],
        in_specs=[vmem, vmem, vmem, smem, smem],
        out_specs=[vmem, vmem],
        compiler_params=pltpu.CompilerParams(vmem_limit_bytes=32 * 2**20),
    )(samples, skel, par, ranks, owners)
    return interp, placed


def solution(mesh):
    placed = (P(None, "dev"), P("dev", None), P(), P(), P())
    return jax.shard_map(
        body,
        mesh=mesh,
        in_specs=placed,
        out_specs=(P(("grp", "dev"), None), P("grp", None, "dev", None)),
        check_vma=False,
    )
```

time: 355 us -> 99.4 us (0.28); the launches traced: 349 us -> 98.6 us
  matrix products: 100 us -> 0 us
  Pallas kernels: 0 us -> 94.3 us
  local copies, waits for them, and re-layouts: 64.6 us -> 3.6 us
  waiting for transfers between devices: 60.1 us -> 0 us
  other arithmetic: 59.7 us -> 0 us
  starting transfers between devices: 32.5 us -> 0 us
  between operations: 17.2 us -> 0.66 us
  blocking collectives: 12.6 us -> 0 us
    dot_general x37 -> x0, matrix products: 95.6 us -> none  [the longest x32 92.2 us: one_block(): return running + jnp.dot(kernel, sketch, preferred_element_type=jnp.float32)]
    pallas_call x0 -> x2, Pallas kernels: none -> 94.3 us  [the longest x1 82.6 us: body(): pl.pallas_call(sweep_kernel, name='sweep', out_shape=[jax.ShapeDtypeStruc...]
    another operation x9 -> x0, other arithmetic: 54.5 us -> none  [the longest x6 34 us: body(): factor = jnp.linalg.cholesky(gram_mat)]
    all_gather x1 -> x0, waiting for transfers between devices: 43.1 us -> none  [body(): piece = lax.all_gather(omega, 'dev', axis=0, tiled=True)]
    ppermute x6 -> x0, starting transfers between devices: 19.7 us -> none  [shifted(): return lax.ppermute(block, axis, route)]
    unnamed x18 -> x10, local copies, waits for them, and re-layouts: 23 us -> 3.6 us
    transpose x2 -> x0, local copies, waits for them, and re-layouts: 16.9 us -> none  [the longest x1 15.4 us: joined_along(): parts = jnp.moveaxis(parts, 0, dim)]
    all_to_all x2 -> x0, waiting for transfers between devices: 16.3 us -> none  [the longest x1 16.3 us: copy_for_each(): return lax.all_to_all(copies, axis, split_axis=0, concat_axis=0, tiled=True)]
  transfers between devices with their start and end apart: 9 -> 0, of which waited for: 2 -> 0; matrix products, arithmetic and copies ran while one was open for 36% -> 0% of each run, Pallas kernels for 0% -> 0%
where the time goes in v1:
time: 99.4 us; the launch traced here: 98.6 us
  Pallas kernels  94.3 us (95%)
  local copies, waits for them, and re-layouts  3.6 us (4%)
    pallas_call x1, Pallas kernels, body(): pl.pallas_call(sweep_kernel, name='sweep', out_shape=[jax.ShapeDtypeStruc...  82.6 us
    pallas_call x1, Pallas kernels, body(): pl.pallas_call(solve_kernel, name='solve', out_shape=[jax.ShapeDtypeStruc...  11.7 us
    unnamed x10, local copies, waits for them, and re-layouts  3.6 us

profile of v1, /device:TPU:2, one launch (start us, length us, event | category | flops | bytes accessed | tf_op | source)
XLA Modules:
  0.0 98.6 jit_solution(5118115724402788184)
XLA Ops:
  0.6 82.6 %sweep.1 = (f32[512,256]{1,0:T(8,128)}, f32[256,256]{1,0:T(8,128)}, f32[16,16,256]{2,1,0:T(8,128)}) custom-call(f32[3,2048]{1,0:T(4,128)} %pts.1, bf16[2048,256]{1,0:T(8,128)(2,1)} %om_in.1, s32[32,256]{1,0:T(8,128)} %pivots.1, s32[32]{0:T(128)} %ranks.3), custom_call_target="tpu_custom_call" | custom-call | tf_op jit(solution)/shard_map/sweep/pallas_call | solution.py:477
  83.3 0.0 copy-start.3
  83.3 0.0 copy-start.4
  83.3 0.6 copy-done.3
  83.9 0.0 copy-done.4
  83.9 0.0 copy-start
  83.9 1.0 %copy-done = f32[512,256]{1,0:T(8,128)S(1)} copy-done((f32[512,256]{1,0:T(8,128)S(1)}, f32[512,256]{1,0:T(8,128)}, u32[]{:S(2)}) %copy-start) | copy-done | bytes 524312
  85.0 0.0 copy-start.1
  85.0 0.9 copy-done.1
  85.9 0.0 copy-start.2
  85.9 0.9 copy-done.2
  86.9 11.7 %solve.1 = (f32[512,256]{1,0:T(8,128)}, f32[1,8,16,256]{3,2,1,0:T(8,128)}) custom-call(f32[512,256]{1,0:T(8,128)S(1)} %copy-done, f32[256,256]{1,0:T(8,128)S(1)} %copy-done.1, f32[16,16,256]{2,1,0:T(8,128)S(1)} %copy-done.2, s32[32]{0:T(128)S(1)} %copy-done.3, s32[16]{0:T(128)S(1)} %copy-done.4), custom_call_target="tpu_custom_call" | custom-call | tf_op jit(solution)/shard_map/solve/pallas_call | solution.py:511
Async XLA Ops:
  83.3 0.7 copy-start.3
  83.3 0.7 copy-start.4
  83.9 1.0 %copy-start = (f32[512,256]{1,0:T(8,128)S(1)}, f32[512,256]{1,0:T(8,128)}, u32[]{:S(2)}) copy-start(f32[512,256]{1,0:T(8,128)} %get-tuple-element.5.samples) | copy-start | bytes 1572868
  85.0 0.9 copy-start.1
  85.9 0.9 copy-start.2

commit v2 on v1

--- a/solution.py
+++ b/solution.py
@@ -70,10 +70,47 @@
     return jnp.concatenate([block - 0.5, jnp.zeros((5, n), F32)], axis=0)
 
 
+def hdot(a, b, dims):
+    return lax.dot_general(a, b, (dims, ((), ())), precision=HIGHEST, preferred_element_type=F32)
+
+
+def dot3(a, b, dims):
+    def one(p, q):
+        return lax.dot_general(p, q, (dims, ((), ())), preferred_element_type=F32)
+
+    ah, bh = a.astype(BF), b.astype(BF)
+    al, bl = (a - ah.astype(F32)).astype(BF), (b - bh.astype(F32)).astype(BF)
+    return one(ah, bh) + (one(ah, bl) + one(al, bh))
+
+
+def interp_basis(rows, rank):
+    gram = hdot(rows, rows, ((1,), (1,)))
+    squares = jnp.sum(rows * rows, axis=1, keepdims=True)
+    trace = jnp.sum(squares, axis=0, keepdims=True)
+    low = 0.1 * trace / rank + 1e-06
+    eye = lax.broadcasted_iota(jnp.int32, (RMAX, RMAX), 0) == lax.broadcasted_iota(jnp.int32, (RMAX, RMAX), 1)
+    gram = gram + jnp.where(eye, low, 0.0)
+    high = low + trace
+    a = 2.0 / (low + high)
+    ratio = low / high
+    inv = None
+    for step in range(9):
+        gap = (1.0 - ratio) / (1.0 + ratio)
+        grow = 2.0 / (2.0 - gap * gap)
+        if inv is None:
+            inv = grow * (jnp.where(eye, 2.0 * a, 0.0) - a * a * gram)
+        else:
+            mul = dot3 if step < 6 else hdot
+            prod = mul(gram, inv, ((1,), (0,)))
+            inv = grow * mul(inv, jnp.where(eye, 2.0, 0.0) - prod, ((1,), (0,)))
+        ratio = 1.0 - gap * gap
+    return hdot(inv, rows, ((1,), (0,)))
+
+
 def sweep_kernel(
-    pts, om_in, pivots, ranks,
-    s_out, skel_out, par_out,
-    cp, rp, om, arow, apiv, bcol, acc, accp, kb0, kb1, sbuf, rbuf, prbuf, skel, red, par,
+    pts, om_in, pivots, ranks, owners,
+    interp, placed,
+    packed, outbox, inbox, cp, om, arow, apiv, bcol, acc, accp, kb0, kb1, sbuf, rbuf, prbuf, skel, red, par,
     own_sem, cps, cpr, rps, rpr, oms, omr, fws, rds, rdr, pvs, pvr, sks, skr, pas, par_sem,
 ):
     y, z, x, c = place()
@@ -100,13 +137,31 @@
             pl.semaphore_signal(
                 barrier, inc=1, device_id=to(dev_of(zs, z, x // 2), (y + gy) % 4), device_id_type=MESH
             )
-    cp[0] = pts[...]
+
+    whole = centred(pts[...])
+    packed[...] = whole[:, :HALF] + pltpu.roll(whole[:, HALF:], 3, 0)
+    split = jnp.concatenate([*splits(whole), jnp.zeros((8, LEAF), F32)], axis=0).astype(BF)
+    wanted = pivots[pl.ds(me, 1), :]
+    here = lax.broadcasted_iota(jnp.int32, (LEAF, RMAX), 0) == wanted
+    hit = jnp.dot(split, here.astype(BF), preferred_element_type=F32)
+    picked = hit[0:8] + hit[8:16] + hit[16:24]
+    first64 = lax.broadcasted_iota(jnp.int32, (8, 128), 1) < 64
+    for i in range(2):
+        tile = picked[:, i * 128 : (i + 1) * 128]
+        other = pltpu.roll(tile, 64, 1)
+        for core in range(2):
+            lo = (2 * i + core) * SLAB
+            outbox[i, core, :, : SLAB // 2] = whole[:, lo : lo + SLAB // 2] + pltpu.roll(
+                whole[:, lo + SLAB // 2 : lo + SLAB], 3, 0
+            )
+            outbox[i, core, :, SLAB // 2 :] = jnp.where(first64, tile, other) if core == 0 else jnp.where(first64, other, tile)
+    bcol[0] = distance_rows(whole, True).astype(BF)
     pl.semaphore_wait(barrier, 43)
 
     def row_copy(i, j, core):
         xr, zr = 2 * c + i, x
         return pltpu.make_async_remote_copy(
-            src_ref=pts, dst_ref=rp.at[j], send_sem=rps.at[i * 8 + j * 2 + core], recv_sem=rpr.at[j],
+            src_ref=outbox.at[i, core], dst_ref=inbox.at[j], send_sem=rps.at[i * 8 + j * 2 + core], recv_sem=rpr.at[j],
             device_id=to(dev_of(zr - 2 * (j % 2) + 4, xr - j + 4, core)), device_id_type=MESH,
         )
 
@@ -122,7 +177,7 @@
 
                     @pl.when(self_target)
                     def _():
-                        pltpu.make_async_copy(pts, rp.at[j], rpr.at[j]).start()
+                        pltpu.make_async_copy(outbox.at[i, core], inbox.at[j], rpr.at[j]).start()
 
                     @pl.when(jnp.logical_not(self_target))
                     def _():
@@ -131,7 +186,7 @@
     def col_copies():
         copies = [
             pltpu.make_async_remote_copy(
-                src_ref=pts, dst_ref=cp.at[1], send_sem=cps.at[0], recv_sem=cpr.at[1],
+                src_ref=packed, dst_ref=cp.at[1], send_sem=cps.at[0], recv_sem=cpr.at[1],
                 device_id=to(dev_of(z, x, 1 - c)), device_id_type=MESH,
             )
         ]
@@ -140,7 +195,7 @@
                 core = c if other == 0 else 1 - c
                 copies.append(
                     pltpu.make_async_remote_copy(
-                        src_ref=pts, dst_ref=cp.at[2 + 2 * i + other],
+                        src_ref=packed, dst_ref=cp.at[2 + 2 * i + other],
                         send_sem=cps.at[1 + 2 * i + other], recv_sem=cpr.at[2 + 2 * i + other],
                         device_id=to(dev_of(z - dz + 4, x - dx + 4, core)), device_id_type=MESH,
                     )
@@ -178,32 +233,27 @@
         rows = pl.ds(half * HALF, HALF)
         pltpu.make_async_copy(om.at[slot, rows], om.at[slot, rows], omr.at[slot, half]).wait()
 
+    xyz = lax.broadcasted_iota(jnp.int32, (8, 1), 0) < 3
+
     def build_col(slot):
-        bcol[slot] = distance_rows(centred(cp[slot]), True).astype(BF)
-
-    build_col(0)
-
-    pick_acc = [jnp.zeros((8, 128), F32), jnp.zeros((8, 128), F32)]
+        pltpu.make_async_copy(cp.at[slot], cp.at[slot], cpr.at[slot]).wait()
+        both = cp[slot]
+        for h in range(2):
+            coords = jnp.where(xyz, both if h == 0 else pltpu.roll(both, 5, 0), 0.0)
+            bcol[slot, :, h * HALF : (h + 1) * HALF] = distance_rows(coords, True).astype(BF)
+
+    pick = [None, None]
     for j in range(WAYS):
-        pltpu.make_async_copy(rp.at[j], rp.at[j], rpr.at[j]).wait()
-        xr, zr = block_chip(j)
-        start = pl.multiple_of(((xr % 2) * 2 + c) * SLAB, SLAB)
-        arow[j] = distance_rows(centred(rp[j, :, pl.ds(start, SLAB)]), False).T.astype(BF)
-        whole = centred(rp[j])
-        split = jnp.concatenate([*splits(whole), jnp.zeros((8, LEAF), F32)], axis=0).astype(BF)
-        piv = jnp.broadcast_to(pivots[pl.ds(block_leaf(j), 1), :], (8, RMAX))
-        piv = jnp.where(xr % 2 == 0, piv[:, :128], piv[:, 128:])
-        piv = jnp.where(c == j % 2, piv, pltpu.roll(piv, 64, 1))
-        lane = lax.broadcasted_iota(jnp.int32, (8, 128), 1)
-        piv = jnp.where(lane // 64 == j % 2, piv, -1)
-        here = lax.broadcasted_iota(jnp.int32, (LEAF, 128), 0) == piv[:1]
-        hit = jnp.dot(split, here.astype(BF), preferred_element_type=F32)
-        pick_acc[j // 2] = pick_acc[j // 2] + (hit[0:8] + hit[8:16] + hit[16:24])
+        pltpu.make_async_copy(inbox.at[j], inbox.at[j], rpr.at[j]).wait()
+        got = inbox[j]
+        pair = got[:, : SLAB // 2]
+        coords = jnp.concatenate([jnp.where(xyz, pair, 0.0), jnp.where(xyz, pltpu.roll(pair, 5, 0), 0.0)], axis=1)
+        arow[j] = distance_rows(coords, False).T.astype(BF)
+        points = got[:, SLAB // 2 :]
+        pick[j // 2] = points if j % 2 == 0 else jnp.where(first64, pick[j // 2], points)
     for t in range(2):
-        apiv[t * 128 : (t + 1) * 128] = distance_rows(pick_acc[t], False).T.astype(BF)
-    for slot in range(1, 8):
-        pltpu.make_async_copy(cp.at[slot], cp.at[slot], cpr.at[slot]).wait()
-        build_col(slot)
+        apiv[t * 128 : (t + 1) * 128] = distance_rows(pick[t], False).T.astype(BF)
+    build_col(1)
     own_copy.wait()
 
     acc[...] = jnp.zeros_like(acc)
@@ -259,6 +309,15 @@
         def _():
             ready(i)
 
+            @pl.when(jnp.logical_and(i >= 3, i < 9))
+            def _():
+                build_col(nth(i + 1)[0])
+
+        @pl.when(t == 16)
+        def _():
+            for late in range(10, 13):
+                ready(jnp.int32(late))
+
         gen(arow[j + 1], slot, half, kb1)
         use_main(slot, half, j, kb0)
         nxt = jnp.minimum(t + 1, 19)
@@ -266,8 +325,6 @@
         gen(arow[(nxt % 2) * 2], nslot, nhalf, kb0)
         use_main(slot, half, j + 1, kb1)
 
-    for i in range(10, 13):
-        ready(jnp.int32(i))
     kp0, kp1 = kb0.at[pl.ds(0, RMAX)], kb1.at[pl.ds(0, RMAX)]
 
     def use_piv(slot, half, kb):
@@ -363,11 +420,15 @@
                     def _():
                         par_send(k, g).start()
 
+    def turn(t):
+        k = t // 3
+        return jnp.where(k < 2, 1 + 2 * k, 2 * (3 - k))
+
     gen(arow[1], 2, 1, kb0)
 
     @pl.loop(0, 12)
     def _(t):
-        j = (t // 3 + 1) % 4
+        j = turn(t)
         i = 10 + 2 * (t % 3)
 
         @pl.when(t == 4)
@@ -380,23 +441,33 @@
         use_main(slot, half, j, kb0)
         nxt = jnp.minimum(t + 1, 11)
         slot2, half2 = nth(10 + 2 * (nxt % 3))
-        gen(arow[(nxt // 3 + 1) % 4], slot2, half2, kb0)
+        gen(arow[turn(nxt)], slot2, half2, kb0)
         use_main(slot1, half1, j, kb1)
-        for jj in range(1, WAYS):
-            @pl.when(t == 3 * jj - 1)
+        for jj, last in ((1, 2), (3, 5), (2, 8)):
+            @pl.when(t == last)
             def _():
                 sbuf[jj - 1] = acc[jj].astype(BF)
                 main_send(jj).start()
 
+    for k in range(3):
+        pltpu.make_async_copy(skel.at[pl.ds(0, PIECE)], skel.at[pl.ds(0, PIECE)], skr.at[k]).wait()
+    basis = interp_basis(skel[...], ranks[block_leaf(0)].astype(F32))
+
+    for q in range(16):
+        pltpu.make_async_copy(par.at[q], par.at[q], par_sem.at[q]).wait()
+    count = jnp.int32(0)
+    source = [jnp.int32(-1)] * 8
+    for q in range(16):
+        mine = owners[q] == y
+        source = [jnp.where(jnp.logical_and(mine, count == k), q, source[k]) for k in range(8)]
+        count = count + jnp.where(mine, 1, 0)
+    for k in range(8):
+        placed[0, k] = jnp.where(source[k] >= 0, par[jnp.maximum(source[k], 0)], 0.0)
+
     for j in range(3):
         pltpu.make_async_copy(rbuf.at[j], rbuf.at[j], rdr.at[j]).wait()
-    s_out[...] = acc[0] + (rbuf[0].astype(F32) + rbuf[1].astype(F32)) + rbuf[2].astype(F32)
-    for k in range(3):
-        pltpu.make_async_copy(skel.at[pl.ds(0, PIECE)], skel.at[pl.ds(0, PIECE)], skr.at[k]).wait()
-    skel_out[...] = skel[...]
-    for q in range(16):
-        pltpu.make_async_copy(par.at[q], par.at[q], par_sem.at[q]).wait()
-    par_out[...] = par[...]
+    samples = acc[0] + (rbuf[0].astype(F32) + rbuf[1].astype(F32)) + rbuf[2].astype(F32)
+    interp[...] = dot3(samples, basis, ((1,), (1,)))
 
     @pl.when(z == y)
     def _():
@@ -429,64 +500,24 @@
                     par_send(k, g).wait_send()
 
 
-def hdot(a, b, dims):
-    return lax.dot_general(a, b, (dims, ((), ())), precision=HIGHEST, preferred_element_type=F32)
-
-
-def solve_kernel(samples, skel, par, ranks, owners, interp, placed):
-    y, z, x, c = place()
-    rows = skel[...]
-    gram = hdot(rows, rows, ((1,), (1,)))
-    squares = jnp.sum(rows * rows, axis=1, keepdims=True)
-    trace = jnp.sum(squares, axis=0, keepdims=True)
-    rank = ranks[y * 8 + 2 * z + x // 2].astype(F32)
-    low = 0.1 * trace / rank + 1e-06
-    eye = lax.broadcasted_iota(jnp.int32, (RMAX, RMAX), 0) == lax.broadcasted_iota(jnp.int32, (RMAX, RMAX), 1)
-    gram = gram + jnp.where(eye, low, 0.0)
-    high = low + trace
-    a = 2.0 / (low + high)
-    ratio = low / high
-    inv = None
-    for step in range(9):
-        gap = (1.0 - ratio) / (1.0 + ratio)
-        grow = 2.0 / (2.0 - gap * gap)
-        if inv is None:
-            inv = grow * (jnp.where(eye, 2.0 * a, 0.0) - a * a * gram)
-        else:
-            prod = hdot(gram, inv, ((1,), (0,)))
-            inv = grow * hdot(inv, jnp.where(eye, 2.0, 0.0) - prod, ((1,), (0,)))
-        ratio = 1.0 - gap * gap
-    basis = hdot(inv, rows, ((1,), (0,)))
-    interp[...] = hdot(samples[...], basis, ((1,), (1,)))
-    placed[...] = jnp.zeros_like(placed)
-    count = jnp.int32(0)
-    for q in range(16):
-        mine = owners[q] == y
-
-        @pl.when(mine)
-        def _():
-            placed[0, count] = par[q]
-
-        count = count + jnp.where(mine, 1, 0)
-
-
 def body(points, omega, pivots, ranks, owners):
     vmem = pl.BlockSpec(memory_space=pltpu.VMEM)
     smem = pl.BlockSpec(memory_space=pltpu.SMEM)
     dma = pltpu.SemaphoreType.DMA
-    samples, skel, par = pl.pallas_call(
+    interp, placed = pl.pallas_call(
         sweep_kernel,
         name="sweep",
         out_shape=[
-            jax.ShapeDtypeStruct((SLAB, S), F32),
-            jax.ShapeDtypeStruct((RMAX, S), F32),
-            jax.ShapeDtypeStruct((16, 16, S), F32),
+            jax.ShapeDtypeStruct((SLAB, RMAX), F32),
+            jax.ShapeDtypeStruct((1, 8, 16, S), F32),
         ],
-        in_specs=[vmem, pl.BlockSpec(memory_space=pl.ANY), vmem, smem],
-        out_specs=[vmem, vmem, vmem],
+        in_specs=[vmem, pl.BlockSpec(memory_space=pl.ANY), vmem, smem, smem],
+        out_specs=[vmem, vmem],
         scratch_shapes=[
-            pltpu.VMEM((8, 3, LEAF), F32),
-            pltpu.VMEM((4, 3, LEAF), F32),
+            pltpu.VMEM((8, HALF), F32),
+            pltpu.VMEM((2, 2, 8, SLAB // 2 + 128), F32),
+            pltpu.VMEM((4, 8, SLAB // 2 + 128), F32),
+            pltpu.VMEM((8, 8, HALF), F32),
             pltpu.VMEM((8, LEAF, S), BF),
             pltpu.VMEM((4, SLAB, DEPTH), BF),
             pltpu.VMEM((RMAX, DEPTH), BF),
@@ -507,18 +538,7 @@
         compiler_params=pltpu.CompilerParams(
             collective_id=0, has_side_effects=True, vmem_limit_bytes=56 * 2**20
         ),
-    )(points, omega, pivots, ranks)
-    interp, placed = pl.pallas_call(
-        solve_kernel,
-        name="solve",
-        out_shape=[
-            jax.ShapeDtypeStruct((SLAB, RMAX), F32),
-            jax.ShapeDtypeStruct((1, 8, 16, S), F32),
-        ],
-        in_specs=[vmem, vmem, vmem, smem, smem],
-        out_specs=[vmem, vmem],
-        compiler_params=pltpu.CompilerParams(vmem_limit_bytes=32 * 2**20),
-    )(samples, skel, par, ranks, owners)
+    )(points, omega, pivots, ranks, owners)
     return interp, placed
 
 

time: 99.4 us -> 82.7 us (0.83)
  Pallas kernels: 94.3 us -> 79.3 us
  local copies, waits for them, and re-layouts: 3.6 us -> 2.56 us
    pallas_call x1 -> x0, Pallas kernels: 11.7 us -> none  [body(): pl.pallas_call(solve_kernel, name='solve', out_shape=[jax.ShapeDtypeStruc...]
    pallas_call x1, Pallas kernels: 82.6 us -> 79.3 us  [body(): pl.pallas_call(sweep_kernel, name='sweep', out_shape=[jax.ShapeDtypeStruc...]
    unnamed x10 -> x4, local copies, waits for them, and re-layouts: 3.6 us -> 2.56 us
where the time goes in v2:
time: 82.7 us; the launch traced here: 82.5 us
  Pallas kernels  79.3 us (96%)
  local copies, waits for them, and re-layouts  2.56 us (3%)
    pallas_call x1, Pallas kernels, body(): pl.pallas_call(sweep_kernel, name='sweep', out_shape=[jax.ShapeDtypeStruc...  79.3 us
    unnamed x4, local copies, waits for them, and re-layouts  2.56 us

profile of v2, /device:TPU:2, one launch (start us, length us, event | category | flops | bytes accessed | tf_op | source)
XLA Modules:
  0.0 82.5 jit_solution(11436021632310931880)
XLA Ops:
  0.6 79.3 %sweep.1 = (f32[512,256]{1,0:T(8,128)}, f32[1,8,16,256]{3,2,1,0:T(8,128)}) custom-call(f32[3,2048]{1,0:T(4,128)} %pts.1, bf16[2048,256]{1,0:T(8,128)(2,1)} %om_in.1, s32[32,256]{1,0:T(8,128)} %pivots.1, s32[32]{0:T(128)} %ranks.1, s32[16]{0:T(128)} %owners.1), custom_call_target="tpu_custom_call" | custom-call | tf_op jit(solution)/shard_map/sweep/pallas_call | solution.py:507
  80.0 0.0 copy-start
  80.0 1.9 %copy.9 = f32[512,256]{1,0:T(8,128)} copy(f32[512,256]{1,0:T(8,128)} %get-tuple-element.4) | data formatting | bytes 1048576
  81.9 0.0 copy-done
  81.9 0.7 copy.10
Async XLA Ops:
  80.0 1.9 %copy-start = (f32[1,8,16,256]{3,2,1,0:T(8,128)S(1)}, f32[1,8,16,256]{3,2,1,0:T(8,128)}, u32[]{:S(2)}) copy-start(f32[1,8,16,256]{3,2,1,0:T(8,128)} %get-tuple-element.5) | copy-start | bytes 393220

commit v3 on v2

--- a/solution.py
+++ b/solution.py
@@ -20,6 +20,7 @@
 RMAX = 256
 PIECE = 64
 HALF = 1024
+BYMXU = 640
 
 
 def place():
@@ -62,7 +63,7 @@
         else:
             block = jnp.where(row >= 6, 0.0, block)
         blocks.append(block)
-    return jnp.concatenate(blocks, axis=0)
+    return jnp.concatenate(blocks, axis=0), value
 
 
 def centred(block):
@@ -100,7 +101,7 @@
         if inv is None:
             inv = grow * (jnp.where(eye, 2.0 * a, 0.0) - a * a * gram)
         else:
-            mul = dot3 if step < 6 else hdot
+            mul = dot3 if step < 7 else hdot
             prod = mul(gram, inv, ((1,), (0,)))
             inv = grow * mul(inv, jnp.where(eye, 2.0, 0.0) - prod, ((1,), (0,)))
         ratio = 1.0 - gap * gap
@@ -110,7 +111,7 @@
 def sweep_kernel(
     pts, om_in, pivots, ranks, owners,
     interp, placed,
-    packed, outbox, inbox, cp, om, arow, apiv, bcol, acc, accp, kb0, kb1, sbuf, rbuf, prbuf, skel, red, par,
+    packed, outbox, inbox, cp, om, arow, apiv, bcol, rowb, ccol, acc, accp, kw0, kw1, sbuf, rbuf, prbuf, skel, red, par,
     own_sem, cps, cpr, rps, rpr, oms, omr, fws, rds, rdr, pvs, pvr, sks, skr, pas, par_sem,
 ):
     y, z, x, c = place()
@@ -155,7 +156,9 @@
                 whole[:, lo + SLAB // 2 : lo + SLAB], 3, 0
             )
             outbox[i, core, :, SLAB // 2 :] = jnp.where(first64, tile, other) if core == 0 else jnp.where(first64, other, tile)
-    bcol[0] = distance_rows(whole, True).astype(BF)
+    operand, value = distance_rows(whole, True)
+    bcol[0] = operand.astype(BF)
+    ccol[0] = value
     pl.semaphore_wait(barrier, 43)
 
     def row_copy(i, j, core):
@@ -240,7 +243,9 @@
         both = cp[slot]
         for h in range(2):
             coords = jnp.where(xyz, both if h == 0 else pltpu.roll(both, 5, 0), 0.0)
-            bcol[slot, :, h * HALF : (h + 1) * HALF] = distance_rows(coords, True).astype(BF)
+            operand, value = distance_rows(coords, True)
+            bcol[slot, :, h * HALF : (h + 1) * HALF] = operand.astype(BF)
+            ccol[slot, :, h * HALF : (h + 1) * HALF] = value
 
     pick = [None, None]
     for j in range(WAYS):
@@ -248,11 +253,17 @@
         got = inbox[j]
         pair = got[:, : SLAB // 2]
         coords = jnp.concatenate([jnp.where(xyz, pair, 0.0), jnp.where(xyz, pltpu.roll(pair, 5, 0), 0.0)], axis=1)
-        arow[j] = distance_rows(coords, False).T.astype(BF)
+        operand = distance_rows(coords, False)[0].T.astype(BF)
+        arow[j * SLAB : (j + 1) * SLAB] = operand
+        for k in range(4):
+            chosen = (6, 14, 22) if k == 3 else (k, 8 + k, 19 + k)
+            depth = lax.broadcasted_iota(jnp.int32, (DEPTH, 128), 0)
+            ones = jnp.where(depth == chosen[0], 1.0, jnp.where(depth == chosen[1], 1.0, jnp.where(depth == chosen[2], 1.0, 0.0)))
+            rowb[k, j * SLAB : (j + 1) * SLAB] = jnp.dot(operand, ones.astype(BF), preferred_element_type=F32)
         points = got[:, SLAB // 2 :]
         pick[j // 2] = points if j % 2 == 0 else jnp.where(first64, pick[j // 2], points)
     for t in range(2):
-        apiv[t * 128 : (t + 1) * 128] = distance_rows(pick[t], False).T.astype(BF)
+        apiv[t * 128 : (t + 1) * 128] = distance_rows(pick[t], False)[0].T.astype(BF)
     build_col(1)
     own_copy.wait()
 
@@ -273,18 +284,34 @@
         cq = jnp.where(slot % 2 == 0, c, 1 - c)
         return dev_of(zq, xq, cq)
 
-    def gen(rows, slot, half, kb):
+    def gen_piv(slot, half, kb):
         cols = pl.ds(pl.multiple_of(half * HALF, HALF), HALF)
-        dist = jnp.dot(rows, bcol[slot, :, cols], preferred_element_type=F32)
+        dist = jnp.dot(apiv[...], bcol[slot, :, cols], preferred_element_type=F32)
         kb[...] = lax.rsqrt(dist).astype(BF)
+
+    def gen(start, n, slot, half, kb):
+        base = pl.multiple_of(half * HALF, HALF)
+        rows = arow[pl.ds(pl.multiple_of(start, SLAB), n), :]
+        dist = jnp.dot(rows, bcol[slot, :, pl.ds(base, BYMXU)], preferred_element_type=F32)
+        kb[:, :BYMXU] = lax.rsqrt(dist).astype(BF)
+        for r in range(0, n, 8):
+            at = pl.ds(pl.multiple_of(start + r, 8), 8)
+            rx, ry, rz, rn = [rowb[k, at, :] for k in range(4)]
+            for t in range(BYMXU, HALF, 128):
+                cols = pl.ds(pl.multiple_of(base + t, 128), 128)
+                cx, cy, cz, cn = [ccol[slot, k : k + 1, cols] for k in (0, 1, 2, 7)]
+                dist = ((rn + cn) + rx * cx) + (ry * cy + rz * cz)
+                kb[r : r + 8, t : t + 128] = lax.rsqrt(dist).astype(BF)
 
     def product(slot, half, kb):
         rows = pl.ds(pl.multiple_of(half * HALF, HALF), HALF)
         return jnp.dot(kb[...], om[slot, rows, :], preferred_element_type=F32)
 
-    def use_main(slot, half, j, kb):
-        keep = jnp.where(slot_leaf(slot) == block_leaf(j), 0.0, 1.0).astype(F32)
-        acc[j] += keep * product(slot, half, kb)
+    def use_main(slot, half, j, kb, blocks):
+        got = product(slot, half, kb)
+        for e in range(blocks):
+            keep = jnp.where(slot_leaf(slot) == block_leaf(j + e), 0.0, 1.0).astype(F32)
+            acc[pl.ds(pl.multiple_of((j + e) * SLAB, SLAB), SLAB), :] += keep * got[e * SLAB : (e + 1) * SLAB]
 
     def ready(i):
         slot, half = nth(i)
@@ -297,35 +324,30 @@
         def _():
             forward(slot, half).start()
 
-    gen(arow[0], 0, 0, kb0)
-
-    @pl.loop(0, 20)
-    def _(t):
-        i = t // 2
-        j = (t % 2) * 2
+    gen(0, 2 * SLAB, 0, 0, kw0)
+
+    @pl.loop(0, 10)
+    def _(i):
         slot, half = nth(i)
-
-        @pl.when(t % 2 == 0)
+        ready(i)
+
+        @pl.when(jnp.logical_and(i >= 3, i < 9))
         def _():
-            ready(i)
-
-            @pl.when(jnp.logical_and(i >= 3, i < 9))
-            def _():
-                build_col(nth(i + 1)[0])
-
-        @pl.when(t == 16)
+            build_col(nth(i + 1)[0])
+
+        @pl.when(i == 8)
         def _():
             for late in range(10, 13):
                 ready(jnp.int32(late))
 
-        gen(arow[j + 1], slot, half, kb1)
-        use_main(slot, half, j, kb0)
-        nxt = jnp.minimum(t + 1, 19)
-        nslot, nhalf = nth(nxt // 2)
-        gen(arow[(nxt % 2) * 2], nslot, nhalf, kb0)
-        use_main(slot, half, j + 1, kb1)
-
-    kp0, kp1 = kb0.at[pl.ds(0, RMAX)], kb1.at[pl.ds(0, RMAX)]
+        gen(2 * SLAB, 2 * SLAB, slot, half, kw1)
+        use_main(slot, half, 0, kw0, 2)
+        nslot, nhalf = nth(jnp.minimum(i + 1, 9))
+        gen(0, 2 * SLAB, nslot, nhalf, kw0)
+        use_main(slot, half, 2, kw1, 2)
+
+    kp0, kp1 = kw0.at[pl.ds(0, RMAX)], kw1.at[pl.ds(0, RMAX)]
+    kb0, kb1 = kw0.at[pl.ds(0, SLAB)], kw1.at[pl.ds(0, SLAB)]
 
     def use_piv(slot, half, kb):
         got = product(slot, half, kb)
@@ -336,7 +358,7 @@
             accp[j, 0] += jnp.where(jnp.logical_or(own, sib), 0.0, 1.0).astype(F32) * part
             accp[j, 1] += jnp.where(sib, 1.0, 0.0).astype(F32) * part
 
-    gen(apiv[...], 0, 0, kp0)
+    gen_piv(0, 0, kp0)
 
     @pl.loop(0, 8)
     def _(t):
@@ -350,10 +372,10 @@
 
         slot, half = nth(2 * t)
         slot1, half1 = nth(2 * t + 1)
-        gen(apiv[...], slot1, half1, kp1)
+        gen_piv(slot1, half1, kp1)
         use_piv(slot, half, kp0)
         slot2, half2 = nth(jnp.minimum(2 * t + 2, 15))
-        gen(apiv[...], slot2, half2, kp0)
+        gen_piv(slot2, half2, kp0)
         use_piv(slot1, half1, kp1)
 
     def piv_send(j):
@@ -424,7 +446,7 @@
         k = t // 3
         return jnp.where(k < 2, 1 + 2 * k, 2 * (3 - k))
 
-    gen(arow[1], 2, 1, kb0)
+    gen(SLAB, SLAB, 2, 1, kb0)
 
     @pl.loop(0, 12)
     def _(t):
@@ -437,16 +459,16 @@
 
         slot, half = nth(i)
         slot1, half1 = nth(i + 1)
-        gen(arow[j], slot1, half1, kb1)
-        use_main(slot, half, j, kb0)
+        gen(j * SLAB, SLAB, slot1, half1, kb1)
+        use_main(slot, half, j, kb0, 1)
         nxt = jnp.minimum(t + 1, 11)
         slot2, half2 = nth(10 + 2 * (nxt % 3))
-        gen(arow[turn(nxt)], slot2, half2, kb0)
-        use_main(slot1, half1, j, kb1)
+        gen(turn(nxt) * SLAB, SLAB, slot2, half2, kb0)
+        use_main(slot1, half1, j, kb1, 1)
         for jj, last in ((1, 2), (3, 5), (2, 8)):
             @pl.when(t == last)
             def _():
-                sbuf[jj - 1] = acc[jj].astype(BF)
+                sbuf[jj - 1] = acc[jj * SLAB : (jj + 1) * SLAB].astype(BF)
                 main_send(jj).start()
 
     for k in range(3):
@@ -466,7 +488,7 @@
 
     for j in range(3):
         pltpu.make_async_copy(rbuf.at[j], rbuf.at[j], rdr.at[j]).wait()
-    samples = acc[0] + (rbuf[0].astype(F32) + rbuf[1].astype(F32)) + rbuf[2].astype(F32)
+    samples = acc[:SLAB] + (rbuf[0].astype(F32) + rbuf[1].astype(F32)) + rbuf[2].astype(F32)
     interp[...] = dot3(samples, basis, ((1,), (1,)))
 
     @pl.when(z == y)
@@ -519,13 +541,15 @@
             pltpu.VMEM((4, 8, SLAB // 2 + 128), F32),
             pltpu.VMEM((8, 8, HALF), F32),
             pltpu.VMEM((8, LEAF, S), BF),
-            pltpu.VMEM((4, SLAB, DEPTH), BF),
+            pltpu.VMEM((4 * SLAB, DEPTH), BF),
             pltpu.VMEM((RMAX, DEPTH), BF),
             pltpu.VMEM((8, DEPTH, LEAF), BF),
-            pltpu.VMEM((4, SLAB, S), F32),
+            pltpu.VMEM((4, 4 * SLAB, 128), F32),
+            pltpu.VMEM((8, 8, LEAF), F32),
+            pltpu.VMEM((4 * SLAB, S), F32),
             pltpu.VMEM((4, 2, PIECE, S), F32),
-            pltpu.VMEM((SLAB, HALF), BF),
-            pltpu.VMEM((SLAB, HALF), BF),
+            pltpu.VMEM((2 * SLAB, HALF), BF),
+            pltpu.VMEM((2 * SLAB, HALF), BF),
             pltpu.VMEM((3, SLAB, S), BF),
             pltpu.VMEM((3, SLAB, S), BF),
             pltpu.VMEM((3, 2, PIECE, S), F32),

time: 82.7 us -> 82.9 us (level)
  no operation moved by 1% of the time
where the time goes in v3:
time: 82.9 us; the launch traced here: 82.7 us
  Pallas kernels  79.5 us (96%)
  local copies, waits for them, and re-layouts  2.56 us (3%)
    pallas_call x1, Pallas kernels, body(): pl.pallas_call(sweep_kernel, name='sweep', out_shape=[jax.ShapeDtypeStruc...  79.5 us
    unnamed x4, local copies, waits for them, and re-layouts  2.56 us

profile of v3, /device:TPU:2, one launch (start us, length us, event | category | flops | bytes accessed | tf_op | source)
XLA Modules:
  0.0 82.7 jit_solution(10813281653046998793)
XLA Ops:
  0.6 79.5 %sweep.1 = (f32[512,256]{1,0:T(8,128)}, f32[1,8,16,256]{3,2,1,0:T(8,128)}) custom-call(f32[3,2048]{1,0:T(4,128)} %pts.1, bf16[2048,256]{1,0:T(8,128)(2,1)} %om_in.1, s32[32,256]{1,0:T(8,128)} %pivots.1, s32[32]{0:T(128)} %ranks.1, s32[16]{0:T(128)} %owners.1), custom_call_target="tpu_custom_call" | custom-call | tf_op jit(solution)/shard_map/sweep/pallas_call | solution.py:529
  80.2 0.0 copy-start
  80.2 1.9 %copy.9 = f32[512,256]{1,0:T(8,128)} copy(f32[512,256]{1,0:T(8,128)} %get-tuple-element.4) | data formatting | bytes 1048576
  82.1 0.0 copy-done
  82.1 0.7 copy.10
Async XLA Ops:
  80.2 1.9 %copy-start = (f32[1,8,16,256]{3,2,1,0:T(8,128)S(1)}, f32[1,8,16,256]{3,2,1,0:T(8,128)}, u32[]{:S(2)}) copy-start(f32[1,8,16,256]{3,2,1,0:T(8,128)} %get-tuple-element.5) | copy-start | bytes 393220

commit v4 on v3

--- a/solution.py
+++ b/solution.py
@@ -378,15 +378,25 @@
         gen_piv(slot2, half2, kp0)
         use_piv(slot1, half1, kp1)
 
-    def piv_send(j):
+    def piv_send(j, part):
         xr, zr = block_chip(j)
         return pltpu.make_async_remote_copy(
-            src_ref=accp.at[j], dst_ref=prbuf.at[j - 1], send_sem=pvs.at[j - 1], recv_sem=pvr.at[j - 1],
-            device_id=to(dev_of(zr, xr, c)), device_id_type=MESH,
+            src_ref=accp.at[j, part], dst_ref=prbuf.at[j - 1, part], send_sem=pvs.at[j - 1, part],
+            recv_sem=pvr.at[j - 1, part], device_id=to(dev_of(zr, xr, c)), device_id_type=MESH,
+        )
+
+    def has_sibling(px, pz, j):
+        dx, dz = (pz + 2 * (j % 2) - px + 4) % 4, (y - pz + 4) % 4
+        return jnp.logical_or(
+            jnp.logical_and(dz == 0, dx <= 1), jnp.logical_and(dx == 0, jnp.logical_or(dz == 1, dz == 3))
         )
 
     for j in range(1, WAYS):
-        piv_send(j).start()
+        piv_send(j, 0).start()
+
+        @pl.when(has_sibling(x, z, j))
+        def _():
+            piv_send(j, 1).start()
 
     def main_send(j):
         xr, zr = block_chip(j)
@@ -416,13 +426,25 @@
         )
 
     def finish_pivots():
-        for j in range(3):
-            pltpu.make_async_copy(prbuf.at[j], prbuf.at[j], pvr.at[j]).wait()
-        total = accp[0] + prbuf[0] + prbuf[1] + prbuf[2]
+        corr = accp[0, 1]
+        for j in range(1, WAYS):
+            sent = has_sibling((x - j + 4) % 4, (z - 2 * (j % 2) + 4) % 4, j)
+            pltpu.make_async_copy(prbuf.at[j - 1, 0], prbuf.at[j - 1, 0], pvr.at[j - 1, 0]).wait()
+
+            @pl.when(sent)
+            def _():
+                pltpu.make_async_copy(prbuf.at[j - 1, 1], prbuf.at[j - 1, 1], pvr.at[j - 1, 1]).wait()
+
+            @pl.when(jnp.logical_not(sent))
+            def _():
+                prbuf[j - 1, 1] = jnp.zeros((PIECE, S), F32)
+
+            corr = corr + prbuf[j - 1, 1]
+        rest = accp[0, 0] + prbuf[0, 0] + prbuf[1, 0] + prbuf[2, 0]
         ids = lax.broadcasted_iota(jnp.int32, (PIECE, S), 0) + piece * PIECE
         live = ids < ranks[block_leaf(0)]
-        skel[piece_rows, :] = jnp.where(live, total[0] + total[1], 0.0)
-        red[...] = jnp.where(live, total[0], 0.0)
+        skel[piece_rows, :] = jnp.where(live, rest + corr, 0.0)
+        red[...] = jnp.where(live, rest, 0.0)
         for k in range(3):
             skel_send(k).start()
         for k in range(4):
@@ -508,7 +530,12 @@
         for i in range(3):
             forward(2 + 2 * i, half).wait_send()
     for j in range(1, WAYS):
-        piv_send(j).wait_send()
+        piv_send(j, 0).wait_send()
+
+        @pl.when(has_sibling(x, z, j))
+        def _():
+            piv_send(j, 1).wait_send()
+
         main_send(j).wait_send()
     for k in range(3):
         skel_send(k).wait_send()
@@ -557,7 +584,7 @@
             pltpu.VMEM((PIECE, S), F32),
             pltpu.VMEM((16, 16, S), F32),
             dma, dma((7,)), dma((8,)), dma((16,)), dma((4,)), dma((4, 2)), dma((8, 2)), dma((3, 2)),
-            dma((3,)), dma((3,)), dma((3,)), dma((3,)), dma((3,)), dma((3,)), dma((16,)), dma((16,)),
+            dma((3,)), dma((3,)), dma((3, 2)), dma((3, 2)), dma((3,)), dma((3,)), dma((16,)), dma((16,)),
         ],
         compiler_params=pltpu.CompilerParams(
             collective_id=0, has_side_effects=True, vmem_limit_bytes=56 * 2**20

time: 82.9 us -> 82.1 us (level)
  Pallas kernels: 79.5 us -> 78.6 us
    pallas_call x1, Pallas kernels: 79.5 us -> 78.6 us  [body(): pl.pallas_call(sweep_kernel, name='sweep', out_shape=[jax.ShapeDtypeStruc...]
where the time goes in v4:
time: 82.1 us; the launch traced here: 81.9 us
  Pallas kernels  78.6 us (96%)
  local copies, waits for them, and re-layouts  2.56 us (3%)
    pallas_call x1, Pallas kernels, body(): pl.pallas_call(sweep_kernel, name='sweep', out_shape=[jax.ShapeDtypeStruc...  78.6 us
    unnamed x4, local copies, waits for them, and re-layouts  2.56 us

profile of v4, /device:TPU:2, one launch (start us, length us, event | category | flops | bytes accessed | tf_op | source)
XLA Modules:
  0.0 81.9 jit_solution(1873928916495267222)
XLA Ops:
  0.6 78.6 %sweep.1 = (f32[512,256]{1,0:T(8,128)}, f32[1,8,16,256]{3,2,1,0:T(8,128)}) custom-call(f32[3,2048]{1,0:T(4,128)} %pts.1, bf16[2048,256]{1,0:T(8,128)(2,1)} %om_in.1, s32[32,256]{1,0:T(8,128)} %pivots.1, s32[32]{0:T(128)} %ranks.1, s32[16]{0:T(128)} %owners.1), custom_call_target="tpu_custom_call" | custom-call | tf_op jit(solution)/shard_map/sweep/pallas_call | solution.py:556
  79.3 0.0 copy-start
  79.3 1.9 %copy.9 = f32[512,256]{1,0:T(8,128)} copy(f32[512,256]{1,0:T(8,128)} %get-tuple-element.4) | data formatting | bytes 1048576
  81.2 0.0 copy-done
  81.2 0.7 copy.10
Async XLA Ops:
  79.3 1.9 %copy-start = (f32[1,8,16,256]{3,2,1,0:T(8,128)S(1)}, f32[1,8,16,256]{3,2,1,0:T(8,128)}, u32[]{:S(2)}) copy-start(f32[1,8,16,256]{3,2,1,0:T(8,128)} %get-tuple-element.5) | copy-start | bytes 393220
